TPU v7x, 128 devices: a whole 4x4x4 slice. The times are simulated.
128 devices in a mesh: band: 8 (over z_hi, y), lon: 16 (over z_lo, x, core).
Axes of the slice: x: 4, y: 4, z: 4 (z_hi: 2, z_lo: 2; z = z_hi * 2 + z_lo), core: 2. Of those that a mesh axis runs over, the one named last changes fastest.
Arguments:
- latent: bfloat16 [256, 2048, 256], P('band', 'lon'), may hold values from -6 to 6
- row_index: int32 [8, 16, 32], P('band', 'lon'), may hold values from 0 to 31
- interp_weights: bfloat16 [4096, 128, 128], P(('band', 'lon')), may hold values from -0.5 to 0.5
- observation_slot_index: int32 [4096, 128], P(('band', 'lon')), may hold values from 0 to 6
- counts: int32 [4096], P(('band', 'lon')), may hold values from 32 to 128
- targets: bfloat16 [4096, 128, 128], P(('band', 'lon')), may hold values from -6 to 6
- gain: float32 [256], replicated, may hold values from 0.5 to 1.5
- w_in: bfloat16 [256, 512], replicated, may hold values from -0.375 to 0.375
- w_out: bfloat16 [512, 256], replicated, may hold values from -0.25 to 0.25
- head: bfloat16 [256, 128], replicated, may hold values from -0.375 to 0.375
Outputs:
- grad_latent: float32 [256, 2048, 256], P('band', 'lon')
- grad_w_in: float32 [256, 512], replicated
- grad_w_out: float32 [512, 256], replicated
- grad_gain: float32 [256], replicated
- grad_head: float32 [256, 128], replicated
All inputs are finite; a program needn't handle non-finite values.
Results may differ from a plain program's by a relative error of at most 0.007.
Values may be sent and summed in bfloat16 or wider, within the bound.
No kernel may reach another device: no remote copies, remote signals or barrier semaphores. Data moves between devices by JAX's collectives and lax.ppermute only.
A program may use at most 128 MiB of HBM per device.

v0:
```python
import math
import jax
import jax.numpy as jnp
from jax import lax
from jax.sharding import PartitionSpec as P

WINDOW_SLOTS = 7
norm_eps = 1e-05


def padded_2(cells, sides, width):
    for axis, dim in sides:
        count = lax.axis_size(axis)
        head = lax.slice_in_dim(cells, 0, width, axis=dim)
        tail = lax.slice_in_dim(cells, cells.shape[dim] - width, cells.shape[dim], axis=dim)
        cells = jnp.concatenate(
            [
                lax.ppermute(tail, axis, [(i, (i + 1) % count) for i in range(count)]),
                cells,
                lax.ppermute(head, axis, [((i + 1) % count, i) for i in range(count)]),
            ],
            axis=dim,
        )
    return cells


def rounded_slots(values):
    return lax.optimization_barrier(values.astype(jnp.bfloat16))


def padded_mix(padded):
    return padded[:, 1:-1] + 0.5 * (padded[:, :-2] + padded[:, 2:])


def silu_slope(pre_act):
    sigmoid_a = jax.nn.sigmoid(pre_act)
    return sigmoid_a * (1.0 + pre_act * (1.0 - sigmoid_a))


def project_pair(weights, tile_pairs, temporal_weight, channels):
    proj_old = jnp.einsum(
        "bol,blc->boc", weights, tile_pairs[..., :channels], preferred_element_type=jnp.float32
    )
    proj_new = jnp.einsum(
        "bol,blc->boc", weights, tile_pairs[..., channels:], preferred_element_type=jnp.float32
    )
    return ((1.0 - temporal_weight) * proj_old + temporal_weight * proj_new).astype(jnp.bfloat16)


def pull_back(weights, obs_grad, temporal_weight):
    obs_float = obs_grad.astype(jnp.float32)
    back_old = ((1.0 - temporal_weight) * obs_float).astype(jnp.bfloat16)
    back_new = (temporal_weight * obs_float).astype(jnp.bfloat16)
    tile_old = jnp.einsum("bol,boc->blc", weights, back_old, preferred_element_type=jnp.float32)
    tile_new = jnp.einsum("bol,boc->blc", weights, back_new, preferred_element_type=jnp.float32)
    return jnp.concatenate([tile_old, tile_new], axis=-1).astype(jnp.bfloat16)


def decode(obs_latent, live_rows, goals, head, loss_scale):
    blocks, obs_rows, channels = obs_latent.shape
    flat_latent = obs_latent.reshape(-1, channels)
    predicted = jnp.dot(flat_latent, head, preferred_element_type=jnp.float32)
    residual = jnp.where(
        live_rows, predicted - goals.reshape(-1, head.shape[1]).astype(jnp.float32), 0.0
    )
    pred_grad = (residual * loss_scale).astype(jnp.bfloat16)
    head_grad = jnp.einsum("rc,rv->cv", flat_latent, pred_grad, preferred_element_type=jnp.float32)
    obs_grad = jnp.einsum("rv,cv->rc", pred_grad, head, preferred_element_type=jnp.float32).astype(
        jnp.bfloat16
    )
    return (head_grad, obs_grad.reshape(blocks, obs_rows, channels))


def body(
    latent,
    row_index,
    interp_weights,
    observation_slot_index,
    counts,
    targets,
    gain,
    w_in,
    w_out,
    head,
):
    lat_rows, lon_cells, channels = latent.shape
    peer_count = lax.axis_size("lon")
    devices_all = lax.axis_size("band") * peer_count
    blocks = interp_weights.shape[0]
    obs_rows = interp_weights.shape[1]
    per_peer = blocks // peer_count
    padded = padded_2(latent, (("lon", 1),), 1)
    summed = padded_mix(padded.astype(jnp.float32))
    inv_rms = lax.rsqrt(jnp.mean(summed * summed, axis=-1, keepdims=True) + norm_eps)
    normed = (summed * inv_rms * gain).astype(jnp.bfloat16)
    pre_act = jnp.einsum("lmc,ch->lmh", normed, w_in, preferred_element_type=jnp.float32)
    activated = jax.nn.silu(pre_act).astype(jnp.bfloat16)
    advanced = (
        latent.astype(jnp.float32)
        + jnp.einsum("lmh,hc->lmc", activated, w_out, preferred_element_type=jnp.float32)
    ).astype(jnp.bfloat16)
    stacked = jnp.concatenate([latent, advanced], axis=-1)
    requested = row_index.reshape(blocks)
    picked = stacked[requested]
    row_select = (requested[:, None] == jnp.arange(lat_rows, dtype=jnp.int32)[None, :]).astype(
        jnp.bfloat16
    )
    temporal_weight = rounded_slots(observation_slot_index.astype(jnp.float32) / (WINDOW_SLOTS - 1))
    live_flags = jnp.arange(obs_rows, dtype=jnp.int32)[None, :] < counts[:, None]
    live_rows = live_flags.reshape(-1, 1)
    loss_scale = 1.0 / math.sqrt(obs_rows)
    tile_pairs = lax.all_to_all(
        picked.reshape(peer_count, per_peer, lon_cells, 2 * channels),
        "lon",
        split_axis=0,
        concat_axis=0,
        tiled=True,
    )
    local_coef = temporal_weight.reshape(blocks, obs_rows, 1).astype(jnp.float32)
    obs_latent = project_pair(
        interp_weights, tile_pairs.reshape(blocks, lon_cells, 2 * channels), local_coef, channels
    )
    head_grad, obs_grad = decode(obs_latent, live_rows, targets, head, loss_scale)
    tile_grads = pull_back(interp_weights, obs_grad, local_coef)
    returned = lax.all_to_all(
        tile_grads.reshape(peer_count, per_peer, lon_cells, 2 * channels),
        "lon",
        split_axis=0,
        concat_axis=0,
        tiled=True,
    )
    grid_grad = jnp.einsum(
        "br,bx->rx",
        row_select,
        returned.reshape(blocks, lon_cells * 2 * channels),
        preferred_element_type=jnp.float32,
    )
    grid_grad = grid_grad.reshape(lat_rows, lon_cells, 2 * channels)
    grad_adv = grid_grad[..., channels:].astype(jnp.bfloat16)
    grad_out = jnp.einsum("lmh,lmc->hc", activated, grad_adv, preferred_element_type=jnp.float32)
    act_grad = jnp.einsum("lmc,hc->lmh", grad_adv, w_out, preferred_element_type=jnp.float32)
    pre_grad = (act_grad * silu_slope(pre_act)).astype(jnp.bfloat16)
    grad_in = jnp.einsum("lmc,lmh->ch", normed, pre_grad, preferred_element_type=jnp.float32)
    normed_grad = jnp.einsum("lmh,ch->lmc", pre_grad, w_in, preferred_element_type=jnp.float32)
    grad_gain = jnp.sum(normed_grad * summed * inv_rms, axis=(0, 1))
    gained = normed_grad * gain
    summed_grad = inv_rms * (
        gained - summed * inv_rms * inv_rms * jnp.mean(gained * summed, axis=-1, keepdims=True)
    )
    grad_padded = padded_2(summed_grad.astype(jnp.bfloat16), (("lon", 1),), 1).astype(
        summed_grad.dtype
    )
    grad_latent = grid_grad[..., :channels] + grid_grad[..., channels:] + padded_mix(grad_padded)
    totals = lax.psum((grad_in, grad_out, grad_gain, head_grad), ("band", "lon"))
    return (
        grad_latent,
        totals[0] / devices_all,
        totals[1] / devices_all,
        totals[2] / devices_all,
        totals[3] / devices_all,
    )


def solution(mesh):
    return jax.shard_map(
        body,
        mesh=mesh,
        in_specs=(
            P("band", "lon", None),
            P("band", "lon", None),
            P(("band", "lon"), None, None),
            P(("band", "lon"), None),
            P(("band", "lon")),
            P(("band", "lon"), None, None),
            P(),
            P(),
            P(),
            P(),
        ),
        out_specs=(P("band", "lon", None), P(), P(), P(), P()),
        check_vma=False,
    )
```

profile of v0, /device:TPU:1, one launch (start us, length us, event | category | flops | bytes accessed | tf_op | source)
XLA Modules:
  0.0 456.2 jit_solution(16606701495915434797)
XLA Ops:
  7.2 0.0 copy-start
  7.2 2.9 copy.28
  10.1 2.7 collective-permute-start
  12.7 0.0 collective-permute-start.1
  12.8 0.8 collective-permute-done
  13.6 2.6 collective-permute-done.1
  16.2 0.3 maximum_convert_fusion
  16.5 0.0 copy-start.17
  16.5 0.8 multiply_reduce_fusion.2
  17.4 0.0 copy-start.4
  17.4 0.0 copy-start.21
  17.4 0.8 multiply_convert_fusion.5
  18.2 0.3 copy-done.21
  18.5 5.2 %multiply_convert_fusion.1 = (bf16[32,128,512]{2,1,0:T(8,128)(2,1)S(1)}, f32[32,128,512]{2,1,0:T(8,128)}) fusion(bf16[256,512]{1,0:T(8,128)(2,1)S(1)} %copy-done.21, bf16[32,128,256]{2,0,1:T(8,128)(2,1)S(1)} %multiply_convert_fusion.5), kind=kOutput, calls=%fused_computation.2 | convolution fusion | flops 1084227584 | bytes 14942208 | tf_op jit(solution)/shard_map/lmc,ch->lmh/dot_general | solution.py:96
  23.7 1.9 copy-done.10
  25.6 1.3 add_convert_fusion.1
  26.9 2.3 pad_maximum_fusion
  29.2 5.0 %gather_fusion = bf16[32,128,512]{2,1,0:T(8,128)(2,1)} fusion(bf16[32,128,512]{2,1,0:T(8,128)(2,1)} %pad_maximum_fusion, s32[1024]{0:T(1024)S(1)} %pad_clamp_fusion), kind=kCustom, calls=%fused_computation | custom fusion | bytes 8388736 | tf_op jit(solution)/shard_map/gather | solution.py:104
  34.2 6.4 %all-to-all-start = ((bf16[16,2,128,512]{3,2,1,0:T(8,128)(2,1)}), bf16[16,2,128,512]{3,2,1,0:T(8,128)(2,1)}, u32[]{:S(2)}, u32[]{:S(2)}) async-start(bf16[16,2,128,512]{3,2,1,0:T(8,128)(2,1)} %bitcast.68), calls=%async_computation | async-start | bytes 8388608 | tf_op jit(solution)/shard_map/all_to_all | solution.py:112
  40.7 0.1 fusion.41
  40.8 56.3 %all-to-all-done = bf16[16,2,128,512]{3,2,1,0:T(8,128)(2,1)} async-done(((bf16[16,2,128,512]{3,2,1,0:T(8,128)(2,1)}), bf16[16,2,128,512]{3,2,1,0:T(8,128)(2,1)}, u32[]{:S(2)}, u32[]{:S(2)}) %all-to-all-start) | async-done | bytes 4194336 | tf_op jit(solution)/shard_map/all_to_all | solution.py:112
  97.0 2.3 fusion.18
  99.3 0.0 copy-start.15
  99.3 0.0 copy-start.20
  99.4 2.6 add_convert_fusion
  102.0 1.4 copy-done.6
  103.4 2.3 fusion.2
  105.7 1.1 copy-done.8
  106.7 0.7 convolution_convert_fusion
  107.4 3.4 copy.32
  110.9 3.0 fusion.24
  113.9 0.4 copy-done.3
  114.3 2.0 fusion.25
  116.3 3.9 copy.34
  120.3 2.6 copy.35
  122.8 4.6 %pad_maximum_fusion.1 = bf16[16,2,128,512]{3,2,1,0:T(8,128)(2,1)} fusion(bf16[16,2,128,256]{3,2,1,0:T(8,128)(2,1)} %copy.35, bf16[16,2,128,256]{3,2,1,0:T(8,128)(2,1)} %copy.34), kind=kLoop, calls=%fused_computation.21 | loop fusion | flops 8388608 | bytes 8388608 | tf_op jit(solution)/shard_map/concatenate | solution.py:56
  127.5 5.1 %all-to-all-start.1 = ((bf16[16,2,128,512]{3,2,1,0:T(8,128)(2,1)}), bf16[16,2,128,512]{3,2,1,0:T(8,128)(2,1)}, u32[]{:S(2)}, u32[]{:S(2)}) async-start(bf16[16,2,128,512]{3,2,1,0:T(8,128)(2,1)} %pad_maximum_fusion.1), calls=%async_computation.1 | async-start | bytes 8388608 | tf_op jit(solution)/shard_map/all_to_all | solution.py:125
  132.6 0.3 all-reduce.3.cloned.1.call-start
  132.9 1.4 fusion.47
  134.3 54.1 %all-to-all-done.1 = bf16[16,2,128,512]{3,2,1,0:T(8,128)(2,1)} async-done(((bf16[16,2,128,512]{3,2,1,0:T(8,128)(2,1)}), bf16[16,2,128,512]{3,2,1,0:T(8,128)(2,1)}, u32[]{:S(2)}, u32[]{:S(2)}) %all-to-all-start.1) | async-done | bytes 4194336 | tf_op jit(solution)/shard_map/all_to_all | solution.py:125
  188.4 5.4 %fusion.3 = f32[32,128,512]{2,0,1:T(8,128)S(1)} fusion(s32[32]{0:T(128)S(1)} %bitcast.74, bf16[4,8,128,512]{3,2,1,0:T(8,128)(2,1)} %bitcast.28), kind=kOutput, calls=%fused_computation.9 | convolution fusion | flops 134218752 | bytes 12583040 | tf_op jit(solution)/shard_map/br,bx->rx/dot_general | solution.py:132
  193.8 0.3 slice.98
  194.2 4.9 %copy-done.11 = bf16[32,128,512]{2,1,0:T(8,128)(2,1)S(1)} copy-done((bf16[32,128,512]{2,1,0:T(8,128)(2,1)S(1)}, bf16[32,128,512]{2,1,0:T(8,128)(2,1)}, u32[]{:S(2)}) %copy-start.11) | copy-done | bytes 4194328
  199.1 3.6 fusion.32
  202.6 6.6 %multiply_convert_fusion = bf16[32,128,512]{2,1,0:T(8,128)(2,1)S(1)} fusion(f32[32,128,512]{2,1,0:T(8,128)} %get-tuple-element.27, bf16[32,128,256]{2,0,1:T(8,128)(2,1)S(1)} %slice.98, bf16[512,256]{1,0:T(8,128)(2,1)S(1)} %copy-done.14), kind=kOutput, calls=%fused_computation.1 | convolution fusion | flops 1092616192 | bytes 14942208 | tf_op jit(solution)/shard_map/lmc,hc->lmh/dot_general | solution.py:141
  209.2 1.9 copy-done.23
  211.2 3.7 fusion.29
  214.8 8.9 %multiply_reduce_fusion = (f32[256]{0:T(256)S(1)}, f32[32,128]{0,1:T(8,128)S(1)}, f32[32,128,256]{2,0,1:T(8,128)}) fusion(f32[32,128,256]{2,0,1:T(8,128)} %copy-done.4, f32[32,128]{0,1:T(8,128)S(1)} %add_rsqrt_fusion, f32[256]{0:T(256)S(1)} %copy-done.17, bf16[256,512]{1,0:T(8,128)(2,1)S(1)} %copy-done.22, bf16[32,128,512]{2,1,0:T(8,128)(2,1)} %copy-done.23), kind=kOutput, calls=%fused_computation.22 | convolution fusion | flops 1080028928 | bytes 12879872 | tf_op jit(solution)/shard_map/lmh,ch->lmc/dot_general | solution.py:144
  223.7 67.3 %psum.30 = f32[256]{0:T(256)S(1)} all-reduce(f32[256]{0:T(256)S(1)} %get-tuple-element.15), channel_id=1, replica_groups=mesh['band'=8,'lon'=16] {'band','lon'}, use_global_device_ids=true, to_apply=%region_5.6 | all-reduce | flops 256 | bytes 2048 | tf_op jit(solution)/shard_map/psum | solution.py:154
  291.1 4.1 multiply_convert_fusion.2
  295.2 0.7 collective-permute-start.2
  295.9 0.5 collective-permute-start.3
  296.4 0.6 broadcast_multiply_fusion.4
  297.0 0.0 all-reduce.3.cloned.1.call-update
  297.0 0.0 collective-permute-done.2
  297.0 2.0 collective-permute-done.3
  299.1 0.3 maximum_convert_fusion.1
  299.4 0.0 copy-start.1
  299.4 5.1 %fusion.8 = f32[32,128,256]{2,0,1:T(8,128)S(1)} fusion(f32[32,130,256]{2,0,1:T(8,128)S(1)} %maximum_convert_fusion.1, f32[32,128,512]{2,0,1:T(8,128)} %copy-done.2), kind=kLoop, calls=%fused_computation.15 | loop fusion | flops 5242880 | bytes 25165824 | tf_op jit(solution)/shard_map/add | solution.py:153
  304.5 4.4 copy.43
  309.0 135.1 %all-reduce.3.cloned.1.call-done = (f32[256,512]{1,0:T(8,128)}, f32[512,256]{1,0:T(8,128)}, f32[256,128]{1,0:T(8,128)}) async-done(((f32[256,512]{1,0:T(8,128)}, f32[512,256]{1,0:T(8,128)}, f32[256,128]{1,0:T(8,128)}), (f32[256,512]{1,0:T(8,128)}, f32[512,256]{1,0:T(8,128)}, f32[256,128]{1,0:T(8,128)})) %all-reduce.3.cloned.1.call-update) | async-done | bytes 1179664 | tf_op jit(solution)/shard_map/psum | solution.py:154
  444.1 1.9 broadcast_multiply_fusion.1
  445.9 1.6 broadcast_multiply_fusion.2
  447.5 1.9 broadcast_multiply_fusion
  (43 shorter events, 0.1 us)
Async XLA Ops:
  7.2 89.9 %copy-start = (bf16[32,128,128]{2,1,0:T(8,128)(2,1)S(1)}, bf16[32,128,128]{2,1,0:T(8,128)(2,1)}, u32[]{:S(2)}) copy-start(bf16[32,128,128]{2,1,0:T(8,128)(2,1)} %param.12) | copy-start | bytes 3145732
  7.2 5.6 %copy-start.18 = (s32[1,1,32]{2,1,0:T(1,128)S(1)}, s32[1,1,32]{2,1,0:T(1,128)}, u32[]{:S(2)}) copy-start(s32[1,1,32]{2,1,0:T(1,128)} %param.11) | copy-start | bytes 388
  10.1 3.5 collective-permute-start
  12.7 3.5 collective-permute-start.1
  16.5 0.9 copy-start.17
  17.4 6.3 %copy-start.4 = (f32[32,128,256]{2,0,1:T(8,128)}, f32[32,128,256]{2,0,1:T(8,128)S(1)}, u32[]{:S(2)}) copy-start(f32[32,128,256]{2,0,1:T(8,128)S(1)} %get-tuple-element.21) | copy-start | bytes 12582916
  17.4 1.1 copy-start.21
  18.5 5.2 %copy-start.12 = (bf16[32,128,256]{2,0,1:T(8,128)(2,1)}, bf16[32,128,256]{2,0,1:T(8,128)(2,1)S(1)}, u32[]{:S(2)}) copy-start(bf16[32,128,256]{2,0,1:T(8,128)(2,1)S(1)} %multiply_convert_fusion.5) | copy-start | bytes 6291460
  18.5 7.1 %copy-start.5 = (bf16[32,128,256]{2,1,0:T(8,128)(2,1)S(1)}, bf16[32,128,256]{2,1,0:T(8,128)(2,1)}, u32[]{:S(2)}) copy-start(bf16[32,128,256]{2,1,0:T(8,128)(2,1)} %param.10) | copy-start | bytes 6291460
  18.5 7.1 %copy-start.14 = (bf16[512,256]{1,0:T(8,128)(2,1)S(1)}, bf16[512,256]{1,0:T(8,128)(2,1)}, u32[]{:S(2)}) copy-start(bf16[512,256]{1,0:T(8,128)(2,1)} %param.18) | copy-start | bytes 786436
  23.7 1.9 copy-start.10
  34.2 6.5 %copy-start.16 = (s32[32,128]{1,0:T(8,128)S(1)}, s32[32,128]{1,0:T(8,128)}, u32[]{:S(2)}) copy-start(s32[32,128]{1,0:T(8,128)} %param.13) | copy-start | bytes 49156
  34.2 6.5 %copy-start.19 = (s32[32]{0:T(128)S(1)}, s32[32]{0:T(128)}, u32[]{:S(2)}) copy-start(s32[32]{0:T(128)} %param.14) | copy-start | bytes 388
  34.2 62.8 %all-to-all-start = ((bf16[16,2,128,512]{3,2,1,0:T(8,128)(2,1)}), bf16[16,2,128,512]{3,2,1,0:T(8,128)(2,1)}, u32[]{:S(2)}, u32[]{:S(2)}) async-start(bf16[16,2,128,512]{3,2,1,0:T(8,128)(2,1)} %bitcast.68), calls=%async_computation | async-start | bytes 8388608 | tf_op jit(solution)/shard_map/all_to_all | solution.py:112
  99.3 4.1 copy-start.15
  99.3 4.1 copy-start.20
  102.0 1.4 copy-start.6
  105.7 1.1 copy-start.8
  110.9 3.4 copy-start.3
  127.5 5.4 %copy-start.7 = (bf16[32,256,128]{1,2,0:T(8,128)(2,1)S(1)}, bf16[32,256,128]{1,2,0:T(8,128)(2,1)}, u32[]{:S(2)}) copy-start(bf16[32,256,128]{1,2,0:T(8,128)(2,1)} %copy-done.6) | copy-start | bytes 6291460
  127.5 5.4 %copy-start.9 = (bf16[4096,128]{1,0:T(8,128)(2,1)S(1)}, bf16[4096,128]{1,0:T(8,128)(2,1)}, u32[]{:S(2)}) copy-start(bf16[4096,128]{1,0:T(8,128)(2,1)} %copy-done.8) | copy-start | bytes 3145732
  127.5 60.9 %all-to-all-start.1 = ((bf16[16,2,128,512]{3,2,1,0:T(8,128)(2,1)}), bf16[16,2,128,512]{3,2,1,0:T(8,128)(2,1)}, u32[]{:S(2)}, u32[]{:S(2)}) async-start(bf16[16,2,128,512]{3,2,1,0:T(8,128)(2,1)} %pad_maximum_fusion.1), calls=%async_computation.1 | async-start | bytes 8388608 | tf_op jit(solution)/shard_map/all_to_all | solution.py:125
  132.6 311.5 %all-reduce.3.cloned.1.call-start = ((), (), s32[]{:S(2)}) async-start(), calls=%async_computation.2 | async-start | bytes 2359296 | tf_op jit(solution)/shard_map/psum | solution.py:154
  193.8 8.8 %copy-start.2 = (f32[32,128,512]{2,0,1:T(8,128)}, f32[32,128,512]{2,0,1:T(8,128)S(1)}, u32[]{:S(2)}) copy-start(f32[32,128,512]{2,0,1:T(8,128)S(1)} %fusion.3) | copy-start | bytes 25165828
  193.8 5.2 %copy-start.11 = (bf16[32,128,512]{2,1,0:T(8,128)(2,1)S(1)}, bf16[32,128,512]{2,1,0:T(8,128)(2,1)}, u32[]{:S(2)}) copy-start(bf16[32,128,512]{2,1,0:T(8,128)(2,1)} %copy-done.10) | copy-start | bytes 12582916
  202.6 8.5 %copy-start.13 = (bf16[32,128,256]{2,0,1:T(8,128)(2,1)S(1)}, bf16[32,128,256]{2,0,1:T(8,128)(2,1)}, u32[]{:S(2)}) copy-start(bf16[32,128,256]{2,0,1:T(8,128)(2,1)} %copy-done.12) | copy-start | bytes 6291460
  209.2 2.0 copy-start.23
  211.1 3.7 copy-start.22
  295.2 1.8 collective-permute-start.2
  295.9 3.2 collective-permute-start.3
  299.4 150.0 %copy-start.1 = (bf16[32,128,128]{2,1,0:T(8,128)(2,1)S(1)}, bf16[32,128,128]{2,1,0:T(8,128)(2,1)}, u32[]{:S(2)}) copy-start(bf16[32,128,128]{2,1,0:T(8,128)(2,1)} %param.12) | copy-start | bytes 3145732
Sparse Core Ops, SparseCore 0:
  297.2 146.8 all-reduce.2
where the time goes:
time: 457 us; the launch traced here: 456 us
  waiting for transfers between devices  251 us (55%)
  blocking collectives  67.3 us (15%)
  matrix products  48.9 us (11%)
  local copies, waits for them, and re-layouts  34.6 us (8%)
  other arithmetic  24.4 us (5%)
  starting transfers between devices  15.7 us (3%)
  between operations  14.3 us (3%)
    psum x1, waiting for transfers between devices, body(): lax.psum((grad_in, grad_out, grad_gain, head_grad), ('band', 'lon'))  135 us
    psum x1, blocking collectives, body(): lax.psum((grad_in, grad_out, grad_gain, head_grad), ('band', 'lon'))  67.3 us
    all_to_all x1, waiting for transfers between devices, body(): lax.all_to_all(picked.reshape(peer_count, per_peer, lon_cells, 2 * channe...  56.3 us
    all_to_all x1, waiting for transfers between devices, body(): lax.all_to_all(tile_grads.reshape(peer_count, per_peer, lon_cells, 2 * ch...  54.1 us
    unnamed x50, local copies, waits for them, and re-layouts  19.3 us
  transfers between devices with their start and end apart: 7, of which 6 were waited for; matrix products, arithmetic and copies ran while one was open for 3% of the time, Pallas kernels for 0%

commit v1 on v0

--- a/solution.py
+++ b/solution.py
@@ -151,7 +151,7 @@
         summed_grad.dtype
     )
     grad_latent = grid_grad[..., :channels] + grid_grad[..., channels:] + padded_mix(grad_padded)
-    totals = lax.psum((grad_in, grad_out, grad_gain, head_grad), ("band", "lon"))
+    totals = lax.psum(lax.psum((grad_in, grad_out, grad_gain, head_grad), "lon"), "band")
     return (
         grad_latent,
         totals[0] / devices_all,

time: 457 us -> 441 us (0.965)
  blocking collectives: 67.3 us -> 50.8 us
    psum x1 -> x2, blocking collectives: 67.3 us -> 50.8 us  [the longest x1 30.7 us: body(): lax.psum((grad_in, grad_out, grad_gain, head_grad), 'lon')]
    psum x1 -> x2, waiting for transfers between devices: 135 us -> 138 us  [the longest x1 113 us: body(): lax.psum((grad_in, grad_out, grad_gain, head_grad), 'lon')]
    unnamed x50 -> x52, local copies, waits for them, and re-layouts: 19.3 us -> 19.3 us
  transfers between devices with their start and end apart: 7 -> 8, of which waited for: 6 -> 6; matrix products, arithmetic and copies ran while one was open for 3% -> 5% of each run, Pallas kernels for 0% -> 0%
where the time goes in v1:
time: 441 us; the launch traced here: 437 us
  waiting for transfers between devices  252 us (57%)
  blocking collectives  50.8 us (12%)
  matrix products  47.2 us (11%)
  local copies, waits for them, and re-layouts  34.6 us (8%)
  other arithmetic  21.7 us (5%)
  starting transfers between devices  15.9 us (4%)
  between operations  14.4 us (3%)
    psum x1, waiting for transfers between devices, body(): lax.psum((grad_in, grad_out, grad_gain, head_grad), 'lon')  113 us
    all_to_all x1, waiting for transfers between devices, body(): lax.all_to_all(picked.reshape(peer_count, per_peer, lon_cells, 2 * channe...  56.3 us
    all_to_all x1, waiting for transfers between devices, body(): lax.all_to_all(tile_grads.reshape(peer_count, per_peer, lon_cells, 2 * ch...  54.1 us
    psum x1, blocking collectives, body(): lax.psum((grad_in, grad_out, grad_gain, head_grad), 'lon')  30.7 us
    psum x1, waiting for transfers between devices, body(): lax.psum(lax.psum((grad_in, grad_out, grad_gain, head_grad), 'lon'), 'band')  25.5 us
    psum x1, blocking collectives, body(): lax.psum(lax.psum((grad_in, grad_out, grad_gain, head_grad), 'lon'), 'band')  20.1 us
    unnamed x52, local copies, waits for them, and re-layouts  19.3 us
  transfers between devices with their start and end apart: 8, of which 6 were waited for; matrix products, arithmetic and copies ran while one was open for 5% of the time, Pallas kernels for 0%

profile of v1, /device:TPU:1, one launch (start us, length us, event | category | flops | bytes accessed | tf_op | source)
XLA Modules:
  0.0 436.7 jit_solution(12731923982803242846)
XLA Ops:
  7.2 0.0 copy-start
  7.2 2.9 copy.28
  10.1 2.7 collective-permute-start
  12.8 0.8 collective-permute-done
  13.6 2.6 collective-permute-done.1
  16.2 0.3 maximum_convert_fusion
  16.5 0.0 copy-start.18
  16.5 0.8 multiply_reduce_fusion.2
  17.4 0.0 copy-start.4
  17.4 0.0 copy-start.22
  17.4 0.8 multiply_convert_fusion.5
  18.2 0.3 copy-done.22
  18.5 5.2 %multiply_convert_fusion.1 = (bf16[32,128,512]{2,1,0:T(8,128)(2,1)S(1)}, f32[32,128,512]{2,1,0:T(8,128)}) fusion(bf16[256,512]{1,0:T(8,128)(2,1)S(1)} %copy-done.22, bf16[32,128,256]{2,0,1:T(8,128)(2,1)S(1)} %multiply_convert_fusion.5), kind=kOutput, calls=%fused_computation.2 | convolution fusion | flops 1084227584 | bytes 14942208 | tf_op jit(solution)/shard_map/lmc,ch->lmh/dot_general | solution.py:96
  23.7 1.9 copy-done.11
  25.6 1.3 add_convert_fusion.1
  26.9 2.3 pad_maximum_fusion
  29.2 5.0 %gather_fusion = bf16[32,128,512]{2,1,0:T(8,128)(2,1)} fusion(bf16[32,128,512]{2,1,0:T(8,128)(2,1)} %pad_maximum_fusion, s32[1024]{0:T(1024)S(1)} %pad_clamp_fusion), kind=kCustom, calls=%fused_computation | custom fusion | bytes 8388736 | tf_op jit(solution)/shard_map/gather | solution.py:104
  34.2 6.4 %all-to-all-start = ((bf16[16,2,128,512]{3,2,1,0:T(8,128)(2,1)}), bf16[16,2,128,512]{3,2,1,0:T(8,128)(2,1)}, u32[]{:S(2)}, u32[]{:S(2)}) async-start(bf16[16,2,128,512]{3,2,1,0:T(8,128)(2,1)} %bitcast.68), calls=%async_computation | async-start | bytes 8388608 | tf_op jit(solution)/shard_map/all_to_all | solution.py:112
  40.7 0.1 fusion.41
  40.8 56.3 %all-to-all-done = bf16[16,2,128,512]{3,2,1,0:T(8,128)(2,1)} async-done(((bf16[16,2,128,512]{3,2,1,0:T(8,128)(2,1)}), bf16[16,2,128,512]{3,2,1,0:T(8,128)(2,1)}, u32[]{:S(2)}, u32[]{:S(2)}) %all-to-all-start) | async-done | bytes 4194336 | tf_op jit(solution)/shard_map/all_to_all | solution.py:112
  97.0 2.3 fusion.18
  99.3 0.0 copy-start.21
  99.4 2.6 add_convert_fusion
  102.0 1.4 copy-done.7
  103.4 2.3 fusion.2
  105.7 1.1 copy-done.9
  106.7 0.7 convolution_convert_fusion
  107.4 3.4 copy.32
  110.9 3.0 fusion.24
  113.9 0.4 copy-done.3
  114.3 2.0 fusion.25
  116.3 3.9 copy.34
  120.3 2.6 copy.35
  122.8 4.6 %pad_maximum_fusion.1 = bf16[16,2,128,512]{3,2,1,0:T(8,128)(2,1)} fusion(bf16[16,2,128,256]{3,2,1,0:T(8,128)(2,1)} %copy.35, bf16[16,2,128,256]{3,2,1,0:T(8,128)(2,1)} %copy.34), kind=kLoop, calls=%fused_computation.21 | loop fusion | flops 8388608 | bytes 8388608 | tf_op jit(solution)/shard_map/concatenate | solution.py:56
  127.5 5.1 %all-to-all-start.1 = ((bf16[16,2,128,512]{3,2,1,0:T(8,128)(2,1)}), bf16[16,2,128,512]{3,2,1,0:T(8,128)(2,1)}, u32[]{:S(2)}, u32[]{:S(2)}) async-start(bf16[16,2,128,512]{3,2,1,0:T(8,128)(2,1)} %pad_maximum_fusion.1), calls=%async_computation.1 | async-start | bytes 8388608 | tf_op jit(solution)/shard_map/all_to_all | solution.py:125
  132.6 0.3 all-reduce.5.cloned.1.call-start
  132.9 1.4 fusion.47
  134.3 54.1 %all-to-all-done.1 = bf16[16,2,128,512]{3,2,1,0:T(8,128)(2,1)} async-done(((bf16[16,2,128,512]{3,2,1,0:T(8,128)(2,1)}), bf16[16,2,128,512]{3,2,1,0:T(8,128)(2,1)}, u32[]{:S(2)}, u32[]{:S(2)}) %all-to-all-start.1) | async-done | bytes 4194336 | tf_op jit(solution)/shard_map/all_to_all | solution.py:125
  188.4 5.4 %fusion.3 = f32[32,128,512]{2,0,1:T(8,128)S(1)} fusion(s32[32]{0:T(128)S(1)} %bitcast.74, bf16[4,8,128,512]{3,2,1,0:T(8,128)(2,1)} %bitcast.28), kind=kOutput, calls=%fused_computation.9 | convolution fusion | flops 134218752 | bytes 12583040 | tf_op jit(solution)/shard_map/br,bx->rx/dot_general | solution.py:132
  193.8 0.3 slice.98
  194.2 4.9 %copy-done.12 = bf16[32,128,512]{2,1,0:T(8,128)(2,1)S(1)} copy-done((bf16[32,128,512]{2,1,0:T(8,128)(2,1)S(1)}, bf16[32,128,512]{2,1,0:T(8,128)(2,1)}, u32[]{:S(2)}) %copy-start.12) | copy-done | bytes 4194328
  199.1 3.6 fusion.32
  202.6 6.6 %multiply_convert_fusion = bf16[32,128,512]{2,1,0:T(8,128)(2,1)S(1)} fusion(f32[32,128,512]{2,1,0:T(8,128)} %get-tuple-element.30, bf16[32,128,256]{2,0,1:T(8,128)(2,1)S(1)} %slice.98, bf16[512,256]{1,0:T(8,128)(2,1)S(1)} %copy-done.15), kind=kOutput, calls=%fused_computation.1 | convolution fusion | flops 1092616192 | bytes 14942208 | tf_op jit(solution)/shard_map/lmc,hc->lmh/dot_general | solution.py:141
  209.2 1.9 copy-done.24
  211.2 3.7 fusion.29
  214.8 0.0 all-reduce.5.cloned.1.call-update
  214.8 0.3 all-reduce.7.cloned.1.call-start
  215.2 7.2 %multiply_reduce_fusion = (f32[256]{0:T(256)S(1)}, f32[32,128]{0,1:T(8,128)S(1)}, f32[32,128,256]{2,0,1:T(8,128)S(1)}) fusion(f32[32,128,256]{2,0,1:T(8,128)} %copy-done.4, f32[32,128]{0,1:T(8,128)S(1)} %add_rsqrt_fusion, f32[256]{0:T(256)S(1)} %copy-done.18, bf16[256,512]{1,0:T(8,128)(2,1)S(1)} %copy-done.23, bf16[32,128,512]{2,1,0:T(8,128)(2,1)} %copy-done.24), kind=kOutput, calls=%fused_computation.22 | convolution fusion | flops 1080028928 | bytes 12879872 | tf_op jit(solution)/shard_map/lmh,ch->lmc/dot_general | solution.py:144
  222.4 1.6 multiply_convert_fusion.2
  224.1 112.7 %all-reduce.5.cloned.1.call-done = (f32[256,512]{1,0:T(8,128)}, f32[512,256]{1,0:T(8,128)}, f32[256,128]{1,0:T(8,128)}) async-done(((f32[256,512]{1,0:T(8,128)}, f32[512,256]{1,0:T(8,128)}, f32[256,128]{1,0:T(8,128)}), (f32[256,512]{1,0:T(8,128)}, f32[512,256]{1,0:T(8,128)}, f32[256,128]{1,0:T(8,128)})) %all-reduce.5.cloned.1.call-update) | async-done | bytes 1179664 | tf_op jit(solution)/shard_map/psum | solution.py:154
  336.8 0.0 all-reduce.7.cloned.1.call-update
  336.8 0.1 collective-permute-start.2
  336.9 1.0 collective-permute-start.3
  337.9 30.7 %psum.60 = f32[256]{0:T(256)S(1)} all-reduce(f32[256]{0:T(256)S(1)} %get-tuple-element.15), channel_id=1, replica_groups=mesh['band'=8,'lon'=16] {'lon'}, use_global_device_ids=true, to_apply=%region_7.8 | all-reduce | flops 256 | bytes 2048 | tf_op jit(solution)/shard_map/psum | solution.py:154
  368.6 20.1 %psum.61 = f32[256]{0:T(256)S(1)} all-reduce(f32[256]{0:T(256)S(1)} %psum.60), channel_id=1, replica_groups=mesh['band'=8,'lon'=16] {'band'}, use_global_device_ids=true, to_apply=%region_8.9 | all-reduce | flops 256 | bytes 2048 | tf_op jit(solution)/shard_map/psum | solution.py:154
  388.7 0.6 broadcast_multiply_fusion.4
  389.3 0.3 maximum_convert_fusion.1
  389.6 0.0 copy-start.1
  389.7 4.9 %fusion.8 = f32[32,128,256]{2,0,1:T(8,128)S(1)} fusion(f32[32,130,256]{2,0,1:T(8,128)S(1)} %maximum_convert_fusion.1, f32[32,128,512]{2,0,1:T(8,128)} %copy-done.2), kind=kLoop, calls=%fused_computation.15 | loop fusion | flops 5242880 | bytes 25165824 | tf_op jit(solution)/shard_map/add | solution.py:153
  394.6 4.4 %copy.43 = f32[32,128,256]{2,1,0:T(8,128)} copy(f32[32,128,256]{2,0,1:T(8,128)S(1)} %fusion.8) | data formatting | bytes 8388608
  399.0 25.5 %all-reduce.7.cloned.1.call-done = (f32[256,512]{1,0:T(8,128)}, f32[512,256]{1,0:T(8,128)}, f32[256,128]{1,0:T(8,128)}) async-done(((f32[256,512]{1,0:T(8,128)}, f32[512,256]{1,0:T(8,128)}, f32[256,128]{1,0:T(8,128)}), (f32[256,512]{1,0:T(8,128)}, f32[512,256]{1,0:T(8,128)}, f32[256,128]{1,0:T(8,128)})) %all-reduce.7.cloned.1.call-update) | async-done | bytes 1179664 | tf_op jit(solution)/shard_map/psum | solution.py:154
  424.5 1.9 broadcast_multiply_fusion.1
  426.4 1.6 broadcast_multiply_fusion.2
  427.9 1.9 broadcast_multiply_fusion
  (49 shorter events, 0.1 us)
Async XLA Ops:
  7.2 89.9 %copy-start = (bf16[32,128,128]{2,1,0:T(8,128)(2,1)S(1)}, bf16[32,128,128]{2,1,0:T(8,128)(2,1)}, u32[]{:S(2)}) copy-start(bf16[32,128,128]{2,1,0:T(8,128)(2,1)} %param.12) | copy-start | bytes 3145732
  7.2 5.6 %copy-start.19 = (s32[1,1,32]{2,1,0:T(1,128)S(1)}, s32[1,1,32]{2,1,0:T(1,128)}, u32[]{:S(2)}) copy-start(s32[1,1,32]{2,1,0:T(1,128)} %param.11) | copy-start | bytes 388
  10.1 3.5 collective-permute-start
  12.7 3.5 collective-permute-start.1
  16.5 0.9 copy-start.18
  17.4 6.3 %copy-start.4 = (f32[32,128,256]{2,0,1:T(8,128)}, f32[32,128,256]{2,0,1:T(8,128)S(1)}, u32[]{:S(2)}) copy-start(f32[32,128,256]{2,0,1:T(8,128)S(1)} %get-tuple-element.24) | copy-start | bytes 12582916
  17.4 1.1 copy-start.22
  18.5 5.2 %copy-start.13 = (bf16[32,128,256]{2,0,1:T(8,128)(2,1)}, bf16[32,128,256]{2,0,1:T(8,128)(2,1)S(1)}, u32[]{:S(2)}) copy-start(bf16[32,128,256]{2,0,1:T(8,128)(2,1)S(1)} %multiply_convert_fusion.5) | copy-start | bytes 6291460
  18.5 7.1 %copy-start.6 = (bf16[32,128,256]{2,1,0:T(8,128)(2,1)S(1)}, bf16[32,128,256]{2,1,0:T(8,128)(2,1)}, u32[]{:S(2)}) copy-start(bf16[32,128,256]{2,1,0:T(8,128)(2,1)} %param.10) | copy-start | bytes 6291460
  18.5 7.1 %copy-start.15 = (bf16[512,256]{1,0:T(8,128)(2,1)S(1)}, bf16[512,256]{1,0:T(8,128)(2,1)}, u32[]{:S(2)}) copy-start(bf16[512,256]{1,0:T(8,128)(2,1)} %param.18) | copy-start | bytes 786436
  23.7 1.9 copy-start.11
  34.2 6.5 %copy-start.17 = (s32[32,128]{1,0:T(8,128)S(1)}, s32[32,128]{1,0:T(8,128)}, u32[]{:S(2)}) copy-start(s32[32,128]{1,0:T(8,128)} %param.13) | copy-start | bytes 49156
  34.2 6.5 %copy-start.20 = (s32[32]{0:T(128)S(1)}, s32[32]{0:T(128)}, u32[]{:S(2)}) copy-start(s32[32]{0:T(128)} %param.14) | copy-start | bytes 388
  34.2 62.8 %all-to-all-start = ((bf16[16,2,128,512]{3,2,1,0:T(8,128)(2,1)}), bf16[16,2,128,512]{3,2,1,0:T(8,128)(2,1)}, u32[]{:S(2)}, u32[]{:S(2)}) async-start(bf16[16,2,128,512]{3,2,1,0:T(8,128)(2,1)} %bitcast.68), calls=%async_computation | async-start | bytes 8388608 | tf_op jit(solution)/shard_map/all_to_all | solution.py:112
  99.3 4.1 copy-start.16
  99.3 4.1 copy-start.21
  102.0 1.4 copy-start.7
  105.7 1.1 copy-start.9
  110.9 3.4 copy-start.3
  127.5 5.4 %copy-start.8 = (bf16[32,256,128]{1,2,0:T(8,128)(2,1)S(1)}, bf16[32,256,128]{1,2,0:T(8,128)(2,1)}, u32[]{:S(2)}) copy-start(bf16[32,256,128]{1,2,0:T(8,128)(2,1)} %copy-done.7) | copy-start | bytes 6291460
  127.5 5.4 %copy-start.10 = (bf16[4096,128]{1,0:T(8,128)(2,1)S(1)}, bf16[4096,128]{1,0:T(8,128)(2,1)}, u32[]{:S(2)}) copy-start(bf16[4096,128]{1,0:T(8,128)(2,1)} %copy-done.9) | copy-start | bytes 3145732
  127.5 60.9 %all-to-all-start.1 = ((bf16[16,2,128,512]{3,2,1,0:T(8,128)(2,1)}), bf16[16,2,128,512]{3,2,1,0:T(8,128)(2,1)}, u32[]{:S(2)}, u32[]{:S(2)}) async-start(bf16[16,2,128,512]{3,2,1,0:T(8,128)(2,1)} %pad_maximum_fusion.1), calls=%async_computation.1 | async-start | bytes 8388608 | tf_op jit(solution)/shard_map/all_to_all | solution.py:125
  132.6 204.2 %all-reduce.5.cloned.1.call-start = ((), (), s32[]{:S(2)}) async-start(), calls=%async_computation.2 | async-start | bytes 2359296 | tf_op jit(solution)/shard_map/psum | solution.py:154
  193.8 8.8 %copy-start.2 = (f32[32,128,512]{2,0,1:T(8,128)}, f32[32,128,512]{2,0,1:T(8,128)S(1)}, u32[]{:S(2)}) copy-start(f32[32,128,512]{2,0,1:T(8,128)S(1)} %fusion.3) | copy-start | bytes 25165828
  193.8 5.2 %copy-start.12 = (bf16[32,128,512]{2,1,0:T(8,128)(2,1)S(1)}, bf16[32,128,512]{2,1,0:T(8,128)(2,1)}, u32[]{:S(2)}) copy-start(bf16[32,128,512]{2,1,0:T(8,128)(2,1)} %copy-done.11) | copy-start | bytes 12582916
  202.6 8.5 %copy-start.14 = (bf16[32,128,256]{2,0,1:T(8,128)(2,1)S(1)}, bf16[32,128,256]{2,0,1:T(8,128)(2,1)}, u32[]{:S(2)}) copy-start(bf16[32,128,256]{2,0,1:T(8,128)(2,1)} %copy-done.13) | copy-start | bytes 6291460
  209.2 2.0 copy-start.24
  211.1 4.0 copy-start.23
  214.8 209.7 %all-reduce.7.cloned.1.call-start = ((), (), s32[]{:S(2)}) async-start(), calls=%async_computation.3 | async-start | bytes 2359296 | tf_op jit(solution)/shard_map/psum | solution.py:154
  215.2 7.3 %copy-start.5 = (f32[32,128,256]{2,0,1:T(8,128)S(1)}, f32[32,128,256]{2,0,1:T(8,128)}, u32[]{:S(2)}) copy-start(f32[32,128,256]{2,0,1:T(8,128)} %copy-done.4) | copy-start | bytes 12582916
  336.8 52.5 %collective-permute-start.2 = (bf16[32,1,256]{2,0,1:T(8,128)(2,1)S(1)}, bf16[32,1,256]{2,0,1:T(8,128)(2,1)S(1)}, u32[]{:S(2)}, u32[]{:S(2)}) collective-permute-start(bf16[32,1,256]{2,0,1:T(8,128)(2,1)S(1)} %get-tuple-element.25), channel_id=1, source_target_pairs={{0,1},{1,2},{2,3},{3,4},{4,5},{5,6},{6,7},{7,8},{8,9},{9,10},{10,1... | collective-permute-start | bytes 49160 | tf_op jit(solution)/shard_map/ppermute | solution.py:18
  336.9 52.4 %collective-permute-start.3 = (bf16[32,1,256]{2,0,1:T(8,128)(2,1)S(1)}, bf16[32,1,256]{2,0,1:T(8,128)(2,1)S(1)}, u32[]{:S(2)}, u32[]{:S(2)}) collective-permute-start(bf16[32,1,256]{2,0,1:T(8,128)(2,1)S(1)} %get-tuple-element.26), channel_id=1, source_target_pairs={{1,0},{2,1},{3,2},{4,3},{5,4},{6,5},{7,6},{8,7},{9,8},{10,9},{11,1... | collective-permute-start | bytes 49160 | tf_op jit(solution)/shard_map/ppermute | solution.py:20
  389.6 40.2 %copy-start.1 = (bf16[32,128,128]{2,1,0:T(8,128)(2,1)S(1)}, bf16[32,128,128]{2,1,0:T(8,128)(2,1)}, u32[]{:S(2)}) copy-start(bf16[32,128,128]{2,1,0:T(8,128)(2,1)} %param.12) | copy-start | bytes 3145732
Sparse Core Ops, SparseCore 0:
  215.0 121.7 all-reduce.4
  339.5 84.9 all-reduce.6
